TPU v7x, 512 devices: a whole 4x8x8 slice. The times are simulated.
512 devices in a mesh: tile: 128 (over x, z_hi, y, core), depth: 4 (over z_lo).
Axes of the slice: x: 4, y: 8, z: 8 (z_hi: 2, z_lo: 4; z = z_hi * 4 + z_lo), core: 2. Of those that a mesh axis runs over, the one named last changes fastest.
Arguments:
- transmission: float32 [2, 4, 16384, 512], P(None, 'depth', 'tile'), may hold values from -1.2 to 1.2, as said below
- probe_wave: float32 [2, 128, 128], replicated, may hold values from -6 to 6
- fresnel_phase: float32 [128, 128], replicated, may hold values from -3.140625 to 3.140625
- measured: float32 [512, 128, 128], P('tile'), may hold values from 0.1 to 4
- positions: int32 [512, 2], P('tile'), may hold values from 0 to 16383, as said below
- extents: int32 [128, 2], P('tile'), may hold values from 32 to 64
Outputs:
- object_grad: float32 [2, 4, 16384, 512], P(None, 'depth', 'tile')
Inputs may be any that keep to these rules, and one draw needn't show every extreme that they name: `transmission`: real and imaginary parts of a pixel form a complex number of modulus 0.7 to 1.2. `positions`: probe p belongs to tile t = p // 4. Its first row r satisfies ((r - 128 t + 64) mod 16384) - 64 between -64 and 64, both ends reached in every draw; its first column lies between 0 and 384.
All inputs are finite; a program needn't handle non-finite values.
Results may differ from a plain program's by a relative error of at most 0.025.
Values may be sent and summed in bfloat16 or wider, within the bound.
A program may use at most 64 MiB of HBM per device.

v0:
```python
import math

import jax
import jax.numpy as jnp
from jax import lax
from jax.sharding import PartitionSpec as P

BAND = 64


HIGHEST = lax.Precision.HIGHEST


def padded(cells, sides, width):
    for axis, dim in sides:
        count = lax.axis_size(axis)
        head = lax.slice_in_dim(cells, 0, width, axis=dim)
        tail = lax.slice_in_dim(cells, cells.shape[dim] - width, cells.shape[dim], axis=dim)
        cells = jnp.concatenate(
            [
                lax.ppermute(tail, axis, [(i, (i + 1) % count) for i in range(count)]),
                cells,
                lax.ppermute(head, axis, [((i + 1) % count, i) for i in range(count)]),
            ],
            axis=dim,
        )
    return cells


def from_behind(value, axis, by):
    peers = lax.axis_size(axis)
    return lax.ppermute(value, axis, [(i, (i + by) % peers) for i in range(peers)])


def tables(length):
    indices = jnp.arange(length, dtype=jnp.int32)
    product = indices[:, None] * indices[None, :] % length
    angles = product.astype(jnp.float32) * (2.0 * math.pi / length)
    factor = 1.0 / math.sqrt(length)
    return (jnp.cos(angles) * factor, jnp.sin(angles) * factor)


def operators(length):
    cosine, sine_table = tables(length)

    def build_pair(direction):
        left_side = jnp.stack(
            [
                jnp.stack([cosine, direction * sine_table]),
                jnp.stack([-direction * sine_table, cosine]),
            ]
        )
        right_side = jnp.stack(
            [
                jnp.stack([cosine, -direction * sine_table]),
                jnp.stack([direction * sine_table, cosine]),
            ]
        )
        return (left_side, right_side)

    return (build_pair(1.0), build_pair(-1.0))


def transform(real_part, imag_part, matrices):
    stacked = jnp.stack([real_part, imag_part])
    halfway = jnp.einsum("xyab,ypbc->xpac", matrices[0], stacked, precision=HIGHEST)
    finished = jnp.einsum("ypab,yxbc->xpac", halfway, matrices[1], precision=HIGHEST)
    return (finished[0], finished[1])


def propagate(real_part, imag_part, phase_cos, phase_sin, forward_mats, inverse_mats, conjugate):
    spec_real, spec_imag = transform(real_part, imag_part, forward_mats)
    turned_real = spec_real * phase_cos - conjugate * spec_imag * phase_sin
    turned_imag = spec_imag * phase_cos + conjugate * spec_real * phase_sin
    return transform(turned_real, turned_imag, inverse_mats)


def settle(values):
    return lax.optimization_barrier(values.astype(jnp.bfloat16)).astype(jnp.float32)


def shards(transmission, probe_wave, fresnel_phase, measured, positions, extents):
    tile_count = lax.axis_size("tile")
    depth_count = lax.axis_size("depth")
    slab_depth = transmission.shape[1]
    strip_rows = transmission.shape[2]
    columns = transmission.shape[3]
    window = probe_wave.shape[1]
    probe_count = positions.shape[0]
    tile_index = lax.axis_index("tile")
    depth_index = lax.axis_index("depth")
    forward_mats, inverse_mats = operators(window)
    phase_cos = jnp.cos(fresnel_phase)
    phase_sin = jnp.sin(fresnel_phase)
    widened = padded(transmission.astype(jnp.bfloat16), (("tile", 2),), BAND).astype(
        transmission.dtype
    )
    offset = (positions[:, 0] - tile_index * strip_rows + BAND) % (strip_rows * tile_count) - BAND
    start_rows = offset + BAND
    start_cols = positions[:, 1]

    def cut_window(row_start, col_start):
        return lax.dynamic_slice(
            widened, (0, 0, row_start, col_start), (2, slab_depth, window, window)
        )

    windows = jax.vmap(cut_window)(start_rows, start_cols)
    lines = jnp.arange(window, dtype=jnp.int32)
    relative = offset[:, None] + lines[None, :]
    inside = (relative >= -extents[0, 0]) & (relative < strip_rows + extents[0, 1])
    row_mask = inside.astype(jnp.float32)[:, :, None]
    incident_real = probe_wave[0][None] * row_mask
    incident_imag = probe_wave[1][None] * row_mask

    def slab_backward(real_part, imag_part, stored, window_block):
        depth_here = window_block.shape[2]
        gradient_parts = [None] * depth_here
        for slice_index in reversed(range(depth_here)):
            adj_real, adj_imag = propagate(
                real_part, imag_part, phase_cos, phase_sin, forward_mats, inverse_mats, -1.0
            )
            held_real, held_imag = stored[slice_index]
            layer_real = window_block[:, 0, slice_index]
            layer_imag = window_block[:, 1, slice_index]
            gradient_parts[slice_index] = jnp.stack(
                [
                    held_real * adj_real + held_imag * adj_imag,
                    held_real * adj_imag - held_imag * adj_real,
                ]
            )
            real_part = layer_real * adj_real + layer_imag * adj_imag
            imag_part = layer_real * adj_imag - layer_imag * adj_real
        return ((real_part, imag_part), jnp.stack(gradient_parts, axis=1))

    accumulated = jnp.zeros((2, slab_depth, strip_rows + 2 * BAND, columns), jnp.float32)
    share = probe_count // depth_count
    spread_windows = lax.all_to_all(
        windows.astype(jnp.bfloat16), "depth", split_axis=0, concat_axis=2, tiled=True
    ).astype(windows.dtype)
    first_probe = depth_index * share
    real_part = lax.dynamic_slice_in_dim(incident_real, first_probe, share, 0)
    imag_part = lax.dynamic_slice_in_dim(incident_imag, first_probe, share, 0)
    stored_all = []
    for slab_index in range(depth_count):
        block = spread_windows[:, :, slab_index * slab_depth : (slab_index + 1) * slab_depth]
        slab_real_part = real_part
        slab_imag_part = imag_part
        slab_layer_real = block[:, 0, 0]
        slab_layer_imag = block[:, 1, 0]
        slab_stored = [(slab_real_part, slab_imag_part)]
        mixed_real = slab_real_part * slab_layer_real - slab_imag_part * slab_layer_imag
        mixed_imag = slab_real_part * slab_layer_imag + slab_imag_part * slab_layer_real
        slab_real_part, slab_imag_part = propagate(
            mixed_real, mixed_imag, phase_cos, phase_sin, forward_mats, inverse_mats, 1.0
        )
        (real_part, imag_part), stored = ((slab_real_part, slab_imag_part), slab_stored)
        stored_all.append(stored)
        if slab_index + 1 < depth_count:
            real_part = settle(real_part)
            imag_part = settle(imag_part)
    measured_part = lax.dynamic_slice_in_dim(measured, first_probe, share, 0)
    spec_real, spec_imag = transform(real_part, imag_part, forward_mats)
    misfit = spec_real * spec_real + spec_imag * spec_imag - measured_part
    real_part, imag_part = transform(misfit * spec_real, misfit * spec_imag, inverse_mats)
    pieces_all = [None] * depth_count
    for slab_index in reversed(range(depth_count)):
        block = spread_windows[:, :, slab_index * slab_depth : (slab_index + 1) * slab_depth]
        (real_part, imag_part), pieces = slab_backward(
            real_part, imag_part, stored_all[slab_index], block
        )
        pieces_all[slab_index] = pieces
        if slab_index > 0:
            real_part = settle(real_part)
            imag_part = settle(imag_part)
    collected = jnp.concatenate(pieces_all, axis=1)
    returned = lax.all_to_all(
        collected.astype(jnp.bfloat16), "depth", split_axis=1, concat_axis=2, tiled=True
    ).astype(collected.dtype)
    for probe_index in range(probe_count):
        add_row_start = start_rows[probe_index]
        add_col_start = start_cols[probe_index]
        region = lax.dynamic_slice(
            accumulated, (0, 0, add_row_start, add_col_start), (2, slab_depth, window, window)
        )
        accumulated = lax.dynamic_update_slice(
            accumulated, region + returned[:, :, probe_index], (0, 0, add_row_start, add_col_start)
        )
    band_top = accumulated[:, :, :BAND]
    band_bottom = accumulated[:, :, BAND + strip_rows :]
    owned = accumulated[:, :, BAND : BAND + strip_rows]
    from_next = from_behind(band_top.astype(jnp.bfloat16), "tile", -1).astype(band_top.dtype)
    from_prior = from_behind(band_bottom.astype(jnp.bfloat16), "tile", 1).astype(band_bottom.dtype)
    owned = owned.at[:, :, strip_rows - BAND :].add(from_next)
    owned = owned.at[:, :, :BAND].add(from_prior)
    return owned


def solution(mesh):
    placed = (
        P(None, "depth", "tile", None),
        P(),
        P(),
        P("tile", None, None),
        P("tile", None),
        P("tile", None),
    )
    return jax.shard_map(
        shards,
        mesh=mesh,
        in_specs=placed,
        out_specs=P(None, "depth", "tile", None),
        check_vma=False,
    )
```

profile of v0, /device:TPU:128, one launch (start us, length us, event | category | flops | bytes accessed | tf_op | source)
XLA Modules:
  0.0 124.2 jit_solution(7514061871912059032)
XLA Ops:
  0.0 1.1 convert_element_type.279
  1.2 2.1 %collective-permute-start = (bf16[2,1,64,512]{3,2,1,0:T(8,128)(2,1)S(1)}, bf16[2,1,64,512]{3,2,1,0:T(8,128)(2,1)S(1)}, u32[]{:S(2)}, u32[]{:S(2)}) collective-permute-start(bf16[2,1,64,512]{3,2,1,0:T(8,128)(2,1)S(1)} %get-tuple-element.85), channel_id=1, source_target_pairs={{0,4},{4,8},{8,12},{12,16},{16,20},{20,24},{24,28},{28,32},{32,36}... | collective-permute-start | bytes 393224 | tf_op jit(solution)/shard_map/ppermute | solution.py:21
  3.2 13.7 %collective-permute-start.1 = (bf16[2,1,64,512]{3,2,1,0:T(8,128)(2,1)S(1)}, bf16[2,1,64,512]{3,2,1,0:T(8,128)(2,1)S(1)}, u32[]{:S(2)}, u32[]{:S(2)}) collective-permute-start(bf16[2,1,64,512]{3,2,1,0:T(8,128)(2,1)S(1)} %get-tuple-element.86), channel_id=1, source_target_pairs={{4,0},{8,4},{12,8},{16,12},{20,16},{24,20},{28,24},{32,28},{36,32}... | collective-permute-start | bytes 393224 | tf_op jit(solution)/shard_map/ppermute | solution.py:23
  17.2 0.6 copy-done.4
  20.7 10.8 %while.3 = (s32[]{:T(128)}, bf16[2,1,256,512]{3,2,1,0:T(8,128)(2,1)S(1)}, s32[4,4]{1,0:T(4,128)S(1)}, bf16[4,2,1,128,128]{3,4,1,2,0:T(8,128)(2,1)}, s32[]{:T(128)}) while((s32[]{:T(128)}, bf16[2,1,256,512]{3,2,1,0:T(8,128)(2,1)S(1)}, s32[4,4]{1,0:T(4,128)S(1)}, bf16[4,2,1,128,128]{3,4,1,2,0:T(8,128)(2,1)}, s32[]{:T(128)}) %tuple.76), condition=%wide.while_cond.2, body=%wide.while_body.2.sunk | while | flops 2 | bytes 393349 | solution.py:103
  21.3 1.3 %dynamic-slice_bitcast_fusion.2 = bf16[1,2,1,128,128]{4,3,1,2,0:T(8,128)(2,1)S(1)} fusion(bf16[2,1,256,512]{3,2,1,0:T(8,128)(2,1)S(1)} %get-tuple-element.172, s32[]{:T(128)} %bitcast.851, s32[]{:T(128)} %bitcast.852), kind=kLoop, calls=%fused_computation.clone.1 | loop fusion | bytes 131080 | tf_op jit(solution)/shard_map/vmap()/gather
  22.7 0.6 constant_dynamic-update-slice_fusion.2
  24.0 1.3 %dynamic-slice_bitcast_fusion.2 = bf16[1,2,1,128,128]{4,3,1,2,0:T(8,128)(2,1)S(1)} fusion(bf16[2,1,256,512]{3,2,1,0:T(8,128)(2,1)S(1)} %get-tuple-element.172, s32[]{:T(128)} %bitcast.851, s32[]{:T(128)} %bitcast.852), kind=kLoop, calls=%fused_computation.clone.1 | loop fusion | bytes 131080 | tf_op jit(solution)/shard_map/vmap()/gather
  25.5 0.6 constant_dynamic-update-slice_fusion.2
  26.7 1.3 %dynamic-slice_bitcast_fusion.2 = bf16[1,2,1,128,128]{4,3,1,2,0:T(8,128)(2,1)S(1)} fusion(bf16[2,1,256,512]{3,2,1,0:T(8,128)(2,1)S(1)} %get-tuple-element.172, s32[]{:T(128)} %bitcast.851, s32[]{:T(128)} %bitcast.852), kind=kLoop, calls=%fused_computation.clone.1 | loop fusion | bytes 131080 | tf_op jit(solution)/shard_map/vmap()/gather
  28.2 0.6 constant_dynamic-update-slice_fusion.2
  28.8 0.6 fusion.146
  29.4 1.3 %dynamic-slice_bitcast_fusion.2 = bf16[1,2,1,128,128]{4,3,1,2,0:T(8,128)(2,1)S(1)} fusion(bf16[2,1,256,512]{3,2,1,0:T(8,128)(2,1)S(1)} %get-tuple-element.172, s32[]{:T(128)} %bitcast.851, s32[]{:T(128)} %bitcast.852), kind=kLoop, calls=%fused_computation.clone.1 | loop fusion | bytes 131080 | tf_op jit(solution)/shard_map/vmap()/gather
  30.9 0.6 constant_dynamic-update-slice_fusion.2
  31.5 5.6 %all-to-all-start = ((bf16[4,2,1,128,128]{3,4,1,2,0:T(8,128)(2,1)}), bf16[4,2,1,128,128]{3,4,1,2,0:T(8,128)(2,1)S(1)}, u32[]{:S(2)}, u32[]{:S(2)}) async-start(bf16[4,2,1,128,128]{3,4,1,2,0:T(8,128)(2,1)} %get-tuple-element.36), calls=%async_computation | async-start | bytes 524288 | tf_op jit(solution)/shard_map/all_to_all | solution.py:137
  37.2 0.7 copy-done.2
  38.5 3.2 %all-to-all-done = bf16[4,2,1,128,128]{3,4,1,2,0:T(8,128)(2,1)S(1)} async-done(((bf16[4,2,1,128,128]{3,4,1,2,0:T(8,128)(2,1)}), bf16[4,2,1,128,128]{3,4,1,2,0:T(8,128)(2,1)S(1)}, u32[]{:S(2)}, u32[]{:S(2)}) %all-to-all-start) | async-done | bytes 262176 | tf_op jit(solution)/shard_map/all_to_all | solution.py:137
  60.4 0.7 pad_maximum_fusion.2
  61.1 5.6 %all-to-all-start.1 = ((bf16[2,4,1,128,128]{3,4,0,2,1:T(8,128)(2,1)}), bf16[2,4,1,128,128]{3,4,0,2,1:T(8,128)(2,1)S(1)}, u32[]{:S(2)}, u32[]{:S(2)}) async-start(bf16[2,4,1,128,128]{3,4,0,2,1:T(8,128)(2,1)} %pad_maximum_fusion.2), calls=%async_computation.1 | async-start | bytes 524288 | tf_op jit(solution)/shard_map/all_to_all | solution.py:176
  66.7 0.6 fusion.123
  72.3 0.7 fusion.121
  82.8 2.5 %dynamic_update_slice.12 = f32[2,1,256,512]{2,3,0,1:T(8,128)S(1)} dynamic-update-slice(f32[2,1,256,512]{2,3,0,1:T(8,128)S(1)} %broadcast_in_dim.2, f32[2,1,128,128]{2,3,0,1:T(8,128)S(1)} %slice_bitcast_fusion.3, s32[]{:T(128)} %constant.111.clone.1, s32[]{:T(128)} %constant.111.clone.1, s32[]{:T(128)S(6)} %select_n.95, s32[]{:T(128)S(6)} %select_n.96) | dynamic-update-slice | bytes 262148 | tf_op jit(solution)/shard_map/dynamic_update_slice | solution.py:185
  85.4 2.5 %dynamic_update_slice.13 = f32[2,1,256,512]{2,3,0,1:T(8,128)S(1)} dynamic-update-slice(f32[2,1,256,512]{2,3,0,1:T(8,128)S(1)} %dynamic_update_slice.12, f32[2,1,128,128]{2,3,0,1:T(8,128)S(1)} %fusion.12, s32[]{:T(128)} %constant.111.clone.1, s32[]{:T(128)} %constant.111.clone.1, s32[]{:T(128)S(6)} %select_n.97, s32[]{:T(128)S(6)} %select_n.98) | dynamic-update-slice | bytes 262148 | tf_op jit(solution)/shard_map/dynamic_update_slice | solution.py:185
  88.0 2.2 %dynamic_update_slice.14 = f32[2,1,256,512]{2,3,0,1:T(8,128)S(1)} dynamic-update-slice(f32[2,1,256,512]{2,3,0,1:T(8,128)S(1)} %dynamic_update_slice.13, f32[2,1,128,128]{2,3,0,1:T(8,128)S(1)} %fusion.11, s32[]{:T(128)} %constant.111.clone.1, s32[]{:T(128)} %constant.111.clone.1, s32[]{:T(128)S(6)} %select_n.99, s32[]{:T(128)S(6)} %select_n.100) | dynamic-update-slice | bytes 262148 | tf_op jit(solution)/shard_map/dynamic_update_slice | solution.py:185
  90.3 2.5 %dynamic_update_slice.15 = f32[2,1,256,512]{2,3,0,1:T(8,128)S(1)} dynamic-update-slice(f32[2,1,256,512]{2,3,0,1:T(8,128)S(1)} %dynamic_update_slice.14, f32[2,1,128,128]{2,3,0,1:T(8,128)S(1)} %fusion.10, s32[]{:T(128)} %constant.111.clone.1, s32[]{:T(128)} %constant.111.clone.1, s32[]{:T(128)S(6)} %select_n.101, s32[]{:T(128)S(6)} %select_n.102) | dynamic-update-slice | bytes 262148 | tf_op jit(solution)/shard_map/dynamic_update_slice | solution.py:185
  93.0 9.6 %collective-permute-start.2 = (bf16[2,1,64,512]{2,3,0,1:T(8,128)(2,1)S(1)}, bf16[2,1,64,512]{2,3,0,1:T(8,128)(2,1)S(1)}, u32[]{:S(2)}, u32[]{:S(2)}) collective-permute-start(bf16[2,1,64,512]{2,3,0,1:T(8,128)(2,1)S(1)} %get-tuple-element.64), channel_id=1, source_target_pairs={{0,508},{4,0},{8,4},{12,8},{16,12},{20,16},{24,20},{28,24},{32,28}... | collective-permute-start | bytes 393224 | tf_op jit(solution)/shard_map/ppermute | solution.py:32
  102.8 1.9 %collective-permute-start.3 = (bf16[2,1,64,512]{2,3,0,1:T(8,128)(2,1)S(1)}, bf16[2,1,64,512]{2,3,0,1:T(8,128)(2,1)S(1)}, u32[]{:S(2)}, u32[]{:S(2)}) collective-permute-start(bf16[2,1,64,512]{2,3,0,1:T(8,128)(2,1)S(1)} %get-tuple-element.63), channel_id=1, source_target_pairs={{0,4},{4,8},{8,12},{12,16},{16,20},{20,24},{24,28},{28,32},{32,36}... | collective-permute-start | bytes 393224 | tf_op jit(solution)/shard_map/ppermute | solution.py:32
  104.8 2.2 %collective-permute-done.2 = bf16[2,1,64,512]{2,3,0,1:T(8,128)(2,1)S(1)} collective-permute-done((bf16[2,1,64,512]{2,3,0,1:T(8,128)(2,1)S(1)}, bf16[2,1,64,512]{2,3,0,1:T(8,128)(2,1)S(1)}, u32[]{:S(2)}, u32[]{:S(2)}) %collective-permute-start.2) | collective-permute-done | bytes 131104 | tf_op jit(solution)/shard_map/ppermute | solution.py:32
  107.1 2.9 %scatter-add.6 = f32[2,1,128,512]{2,3,0,1:T(8,128)S(1)} dynamic-update-slice(f32[2,1,128,512]{2,3,0,1:T(8,128)S(1)} %slice.421, f32[2,1,64,512]{2,3,0,1:T(8,128)S(1)} %slice_add_fusion.1, s32[]{:T(128)} %constant.111.clone.1, s32[]{:T(128)} %constant.111.clone.1, s32[]{:T(128)} %constant.110.clone.1, s32[]{:T(128)} %constant.111.clone.1) | dynamic-update-slice | bytes 524292 | tf_op jit(solution)/shard_map/scatter-add | solution.py:193
  110.0 11.0 %collective-permute-done.3 = bf16[2,1,64,512]{2,3,0,1:T(8,128)(2,1)S(1)} collective-permute-done((bf16[2,1,64,512]{2,3,0,1:T(8,128)(2,1)S(1)}, bf16[2,1,64,512]{2,3,0,1:T(8,128)(2,1)S(1)}, u32[]{:S(2)}, u32[]{:S(2)}) %collective-permute-start.3) | collective-permute-done | bytes 131104 | tf_op jit(solution)/shard_map/ppermute | solution.py:32
  121.0 2.1 %scatter-add.9 = f32[2,1,128,512]{2,3,0,1:T(8,128)S(1)} dynamic-update-slice(f32[2,1,128,512]{2,3,0,1:T(8,128)S(1)} %scatter-add.6, f32[2,1,64,512]{2,3,0,1:T(8,128)S(1)} %slice_add_fusion, s32[]{:T(128)} %constant.111.clone.1, s32[]{:T(128)} %constant.111.clone.1, s32[]{:T(128)} %constant.111.clone.1, s32[]{:T(128)} %constant.111.clone.1) | dynamic-update-slice | bytes 524292 | tf_op jit(solution)/shard_map/scatter-add | solution.py:194
  123.2 1.0 copy.154
  (119 shorter events, 24.0 us)
Async XLA Ops:
  0.0 20.3 %copy-start = (f32[4,128,128]{2,1,0:T(8,128)S(1)}, f32[4,128,128]{2,1,0:T(8,128)}, u32[]{:S(2)}) copy-start(f32[4,128,128]{2,1,0:T(8,128)} %param.13) | copy-start | bytes 786436
  1.1 18.2 %copy-start.1 = (f32[2,128,128]{2,1,0:T(8,128)S(1)}, f32[2,128,128]{2,1,0:T(8,128)}, u32[]{:S(2)}) copy-start(f32[2,128,128]{2,1,0:T(8,128)} %param.11) | copy-start | bytes 393220
  1.2 19.4 %collective-permute-start = (bf16[2,1,64,512]{3,2,1,0:T(8,128)(2,1)S(1)}, bf16[2,1,64,512]{3,2,1,0:T(8,128)(2,1)S(1)}, u32[]{:S(2)}, u32[]{:S(2)}) collective-permute-start(bf16[2,1,64,512]{3,2,1,0:T(8,128)(2,1)S(1)} %get-tuple-element.85), channel_id=1, source_target_pairs={{0,4},{4,8},{8,12},{12,16},{16,20},{20,24},{24,28},{28,32},{32,36}... | collective-permute-start | bytes 393224 | tf_op jit(solution)/shard_map/ppermute | solution.py:21
  3.2 17.4 %collective-permute-start.1 = (bf16[2,1,64,512]{3,2,1,0:T(8,128)(2,1)S(1)}, bf16[2,1,64,512]{3,2,1,0:T(8,128)(2,1)S(1)}, u32[]{:S(2)}, u32[]{:S(2)}) collective-permute-start(bf16[2,1,64,512]{3,2,1,0:T(8,128)(2,1)S(1)} %get-tuple-element.86), channel_id=1, source_target_pairs={{4,0},{8,4},{12,8},{16,12},{20,16},{24,20},{28,24},{32,28},{36,32}... | collective-permute-start | bytes 393224 | tf_op jit(solution)/shard_map/ppermute | solution.py:23
  17.2 0.7 copy-start.4
  18.4 0.7 copy-start.3
  31.5 10.2 %all-to-all-start = ((bf16[4,2,1,128,128]{3,4,1,2,0:T(8,128)(2,1)}), bf16[4,2,1,128,128]{3,4,1,2,0:T(8,128)(2,1)S(1)}, u32[]{:S(2)}, u32[]{:S(2)}) async-start(bf16[4,2,1,128,128]{3,4,1,2,0:T(8,128)(2,1)} %get-tuple-element.36), calls=%async_computation | async-start | bytes 524288 | tf_op jit(solution)/shard_map/all_to_all | solution.py:137
  37.1 0.8 copy-start.2
  61.1 21.5 %all-to-all-start.1 = ((bf16[2,4,1,128,128]{3,4,0,2,1:T(8,128)(2,1)}), bf16[2,4,1,128,128]{3,4,0,2,1:T(8,128)(2,1)S(1)}, u32[]{:S(2)}, u32[]{:S(2)}) async-start(bf16[2,4,1,128,128]{3,4,0,2,1:T(8,128)(2,1)} %pad_maximum_fusion.2), calls=%async_computation.1 | async-start | bytes 524288 | tf_op jit(solution)/shard_map/all_to_all | solution.py:176
  93.0 14.0 %collective-permute-start.2 = (bf16[2,1,64,512]{2,3,0,1:T(8,128)(2,1)S(1)}, bf16[2,1,64,512]{2,3,0,1:T(8,128)(2,1)S(1)}, u32[]{:S(2)}, u32[]{:S(2)}) collective-permute-start(bf16[2,1,64,512]{2,3,0,1:T(8,128)(2,1)S(1)} %get-tuple-element.64), channel_id=1, source_target_pairs={{0,508},{4,0},{8,4},{12,8},{16,12},{20,16},{24,20},{28,24},{32,28}... | collective-permute-start | bytes 393224 | tf_op jit(solution)/shard_map/ppermute | solution.py:32
  102.8 18.2 %collective-permute-start.3 = (bf16[2,1,64,512]{2,3,0,1:T(8,128)(2,1)S(1)}, bf16[2,1,64,512]{2,3,0,1:T(8,128)(2,1)S(1)}, u32[]{:S(2)}, u32[]{:S(2)}) collective-permute-start(bf16[2,1,64,512]{2,3,0,1:T(8,128)(2,1)S(1)} %get-tuple-element.63), channel_id=1, source_target_pairs={{0,4},{4,8},{8,12},{12,16},{16,20},{20,24},{24,28},{28,32},{32,36}... | collective-permute-start | bytes 393224 | tf_op jit(solution)/shard_map/ppermute | solution.py:32
where the time goes:
time: 125 us; the launch traced here: 124 us
  starting transfers between devices  38.4 us (31%)
  local copies, waits for them, and re-layouts  31.1 us (25%)
  matrix products  17.7 us (14%)
  between operations  16.6 us (13%)
  waiting for transfers between devices  16.5 us (13%)
  other arithmetic  3.86 us (3%)
    ppermute x1, starting transfers between devices, padded(): lax.ppermute(head, axis, [((i + 1) % count, i) for i in range(count)])  13.7 us
    ppermute x2, waiting for transfers between devices, from_behind(): lax.ppermute(value, axis, [(i, (i + by) % peers) for i in range(peers)])  13.3 us
    ppermute x2, starting transfers between devices, from_behind(): lax.ppermute(value, axis, [(i, (i + by) % peers) for i in range(peers)])  11.5 us
    gather x20, local copies, waits for them, and re-layouts  10.8 us
    dot_general x18, matrix products, transform(): jnp.einsum('ypab,yxbc->xpac', halfway, matrices[1], precision=HIGHEST)  10.7 us
    dynamic_update_slice x4, local copies, waits for them, and re-layouts, shards(): lax.dynamic_update_slice(accumulated, region + returned[:, :, probe_index...  9.68 us
    dot_general x18, matrix products, transform(): jnp.einsum('xyab,ypbc->xpac', matrices[0], stacked, precision=HIGHEST)  7.06 us
    all_to_all x1, starting transfers between devices, shards(): lax.all_to_all(collected.astype(jnp.bfloat16), 'depth', split_axis=1, con...  5.59 us
  transfers between devices with their start and end apart: 6, of which 3 were waited for; matrix products, arithmetic and copies ran while one was open for 5% of the time, Pallas kernels for 0%

commit v1 on v0

v1 whole, which is shorter than its diff:
```python
import math

import jax
import jax.numpy as jnp
import numpy as np
from jax import lax
from jax.experimental import pallas as pl
from jax.experimental.pallas import tpu as pltpu
from jax.sharding import PartitionSpec as P

BAND = 64
W = 128
STRIP = 128
OW = 512
BLOCKS = OW // W
DEPTH = 4
F32 = jnp.float32
BF16 = jnp.bfloat16
MESH = pl.DeviceIdType.MESH


def dft_matrices():
    index = np.arange(W)
    angles = (index[:, None] * index[None, :] % W) * (2.0 * math.pi / W)
    cosine = np.cos(angles) / math.sqrt(W)
    sine = np.sin(angles) / math.sqrt(W)
    a = np.block([[cosine, sine], [-sine, cosine]])
    b = a.T
    parts = []
    for m in (a, b):
        high = m.astype(BF16)
        low = (m - high.astype(np.float64)).astype(BF16)
        parts.append((high, low))
    right = np.stack([np.concatenate([h, l, h], axis=0) for h, l in (parts[1], parts[0])])
    left = np.stack([np.concatenate([h, l, h], axis=1) for h, l in (parts[0], parts[1])])
    return right, left


def kernel(
    tile_count,
    pos_ref, ext_ref, tr_hbm, probe_hbm, phase_hbm, meas_hbm, right_hbm, left_hbm,
    out_ref,
    tr, probe, phase, meas, right, left, gcos, gsin, waves,
    halo_send, halo, wsend, wrecv, gsend, grecv, band_send, band_recv,
    local_sem, hs, hr, ws, wr, gs, gr, bs, br,
):
    t = lax.axis_index("tile")
    me = lax.axis_index("depth")
    above = lax.rem(t + tile_count - 1, tile_count)
    below = lax.rem(t + 1, tile_count)
    peers = [lax.rem(me + j, DEPTH) for j in range(1, DEPTH)]

    barrier = pltpu.get_barrier_semaphore()
    pl.semaphore_signal(barrier, inc=1, device_id=(above, me), device_id_type=MESH)
    pl.semaphore_signal(barrier, inc=1, device_id=(below, me), device_id_type=MESH)
    for p in peers:
        pl.semaphore_signal(barrier, inc=1, device_id=(t, p), device_id_type=MESH)

    fetches = [
        pltpu.make_async_copy(tr_hbm.at[:, 0], tr, local_sem.at[0]),
        pltpu.make_async_copy(probe_hbm, probe, local_sem.at[1]),
        pltpu.make_async_copy(phase_hbm, phase, local_sem.at[2]),
        pltpu.make_async_copy(meas_hbm.at[me], meas, local_sem.at[3]),
        pltpu.make_async_copy(right_hbm, right, local_sem.at[4]),
        pltpu.make_async_copy(left_hbm, left, local_sem.at[5]),
    ]
    for f in fetches:
        f.start()

    def offset_of(p):
        rows = STRIP * tile_count
        return lax.rem(pos_ref[p, 0] - t * STRIP + (rows + BAND), rows) - BAND

    offs = [offset_of(p) for p in range(DEPTH)]
    cols = [pos_ref[p, 1] for p in range(DEPTH)]

    half_rows = lax.broadcasted_iota(jnp.int32, (BAND, W), 0)
    half_lanes = lax.broadcasted_iota(jnp.int32, (BAND, W), 1)

    def column_mask(p, m):
        position = half_lanes + m * W
        return (position >= cols[p]) & (position < cols[p] + W)

    def upward(p):
        return (half_rows * 0 + offs[p]) <= 0

    fetches[0].wait()
    for i in range(2):
        halo_send[i] = tr[:, i * BAND:(i + 1) * BAND, :].astype(BF16)

    for p in range(DEPTH):
        up = upward(p)
        for c in range(2):
            total = jnp.zeros((BAND, W), F32)
            for m in range(BLOCKS):
                block = jnp.where(up, tr[c, :BAND, m * W:(m + 1) * W], tr[c, BAND:, m * W:(m + 1) * W])
                total = jnp.where(column_mask(p, m), block, total)
            wsend[0, p, c] = total.astype(BF16)

    pl.semaphore_wait(barrier, 2 + len(peers))

    def halo_copy(i):
        return pltpu.make_async_remote_copy(
            src_ref=halo_send.at[i], dst_ref=halo.at[1 - i],
            send_sem=hs.at[i], recv_sem=hr.at[1 - i],
            device_id=(above if i == 0 else below, me), device_id_type=MESH,
        )

    def window_copy(h, p):
        return pltpu.make_async_remote_copy(
            src_ref=wsend.at[h, p], dst_ref=wrecv.at[h, me],
            send_sem=ws.at[h, p], recv_sem=wr.at[h, me],
            device_id=(t, p), device_id_type=MESH,
        )

    def window_arrival(h, k):
        return pltpu.make_async_remote_copy(
            src_ref=wsend.at[h, k], dst_ref=wrecv.at[h, k],
            send_sem=ws.at[h, k], recv_sem=wr.at[h, k],
            device_id=(t, k), device_id_type=MESH,
        )

    halo_copies = [halo_copy(i) for i in range(2)]
    for c in halo_copies:
        c.start()
    for p in reversed(peers):
        window_copy(0, p).start()
    wrecv[0, me] = wsend[0, me]

    fetches[2].wait()
    gcos[...] = jnp.cos(phase[...])
    gsin[...] = jnp.sin(phase[...])
    my_off = offset_of(me)
    my_col = pos_ref[me, 1]
    rows = lax.broadcasted_iota(jnp.int32, (W, W), 0)
    extended = my_off + ((rows - my_off + W) & (W - 1))
    inside = (extended >= -ext_ref[0, 0]) & (extended < STRIP + ext_ref[0, 1])
    fetches[1].wait()
    for c in range(2):
        turned = pltpu.roll(probe[c], (my_off + W) & (W - 1), 0)
        turned = pltpu.roll(turned, my_col & (W - 1), 1)
        waves[0, c] = jnp.where(inside, turned, 0.0)

    for c in halo_copies:
        c.wait()
    for p in range(DEPTH):
        up = upward(p)
        from_halo = jnp.where(up, half_rows - (BAND + offs[p]), offs[p] - 1 - half_rows) >= 0
        for c in range(2):
            total = jnp.zeros((BAND, W), F32)
            for m in range(BLOCKS):
                lanes = slice(m * W, (m + 1) * W)
                outer = jnp.where(up, halo[0, c, :, lanes].astype(F32), halo[1, c, :, lanes].astype(F32))
                inner = jnp.where(up, tr[c, BAND:, lanes], tr[c, :BAND, lanes])
                block = jnp.where(from_halo, outer, inner)
                total = jnp.where(column_mask(p, m), block, total)
            wsend[1, p, c] = total.astype(BF16)
    for p in reversed(peers):
        window_copy(1, p).start()
    wrecv[1, me] = wsend[1, me]

    for i in (3, 4, 5):
        fetches[i].wait()

    up_me = (half_rows * 0 + my_off) <= 0

    def layer(k):
        both = []
        for c in range(2):
            certain = wrecv[0, k, c].astype(F32)
            mixed = wrecv[1, k, c].astype(F32)
            both.append(jnp.concatenate(
                [jnp.where(up_me, certain, mixed), jnp.where(up_me, mixed, certain)], axis=0))
        return both

    def split(x, exact):
        high = x.astype(BF16)
        if not exact:
            return high, None
        return high, (x - high.astype(F32)).astype(BF16)

    def transform(re, im, inverse, exact):
        d = 1 if inverse else 0
        high, low = split(jnp.concatenate([re, im], axis=1), exact)
        parts = [high, high] + ([low] if exact else [])
        depth = len(parts) * 2 * W
        u = jnp.dot(jnp.concatenate(parts, axis=1), right[d, :depth, :], preferred_element_type=F32)
        high, low = split(jnp.concatenate([u[:, :W], u[:, W:]], axis=0), exact)
        parts = [high, high] + ([low] if exact else [])
        v = jnp.dot(left[d, :, :depth], jnp.concatenate(parts, axis=0), preferred_element_type=F32)
        return v[:W], v[W:]

    def propagate(re, im, conjugate, exact):
        re, im = transform(re, im, False, exact)
        co, si = gcos[...], gsin[...]
        if conjugate:
            re, im = re * co + im * si, im * co - re * si
        else:
            re, im = re * co - im * si, im * co + re * si
        return transform(re, im, True, exact)

    re = im = None
    for k in range(DEPTH):
        for h in range(2):
            @pl.when(me != k)
            def _():
                window_arrival(h, k).wait_recv()
        o_re, o_im = layer(k)
        if k == 0:
            re, im = waves[0, 0], waves[0, 1]
        else:
            waves[k, 0] = re
            waves[k, 1] = im
        re, im = re * o_re - im * o_im, re * o_im + im * o_re
        if k + 1 < DEPTH:
            re, im = propagate(re, im, False, True)
    re, im = transform(re, im, False, True)
    misfit = re * re + im * im - meas[...]
    re, im = transform(misfit * re, misfit * im, True, False)

    up_full = (rows * 0 + my_off) <= 0

    def gradient_copy(k, h):
        return pltpu.make_async_remote_copy(
            src_ref=gsend.at[h, k], dst_ref=grecv.at[h, me],
            send_sem=gs.at[h, k], recv_sem=gr.at[h, me],
            device_id=(t, k), device_id_type=MESH,
        )

    def gradient_arrival(p, h):
        return pltpu.make_async_remote_copy(
            src_ref=gsend.at[h, p], dst_ref=grecv.at[h, p],
            send_sem=gs.at[h, p], recv_sem=gr.at[h, p],
            device_id=(t, p), device_id_type=MESH,
        )

    for k in reversed(range(DEPTH)):
        if k + 1 < DEPTH:
            re, im = propagate(re, im, True, False)
        w_re, w_im = waves[k, 0], waves[k, 1]
        terms = (w_re * re + w_im * im, w_re * im - w_im * re)
        for c in range(2):
            lower, upper = terms[c][:BAND], terms[c][BAND:]
            gsend[1, k, c] = jnp.where(up_me, upper, lower).astype(BF16)
            gsend[0, k, c] = jnp.where(up_me, lower, upper).astype(BF16)

        @pl.when(me != k)
        def _():
            gradient_copy(k, 1).start()
            gradient_copy(k, 0).start()

        @pl.when(me == k)
        def _():
            grecv[1, me] = gsend[1, k]
            grecv[0, me] = gsend[0, k]

        if k > 0:
            o_re, o_im = layer(k)
            re, im = o_re * re + o_im * im, o_re * im - o_im * re

    for p in peers:
        gradient_arrival(p, 1).wait_recv()
    for c in range(2):
        for m in range(BLOCKS):
            lanes = slice(m * W, (m + 1) * W)
            top = bottom = jnp.zeros((BAND, W), F32)
            for p in range(DEPTH):
                up = upward(p)
                from_halo = jnp.where(up, half_rows - (BAND + offs[p]), offs[p] - 1 - half_rows) >= 0
                piece = jnp.where(from_halo & column_mask(p, m), grecv[1, p, c].astype(F32), 0.0)
                top = top + jnp.where(up, piece, 0.0)
                bottom = bottom + jnp.where(up, 0.0, piece)
            band_send[0, c, :, lanes] = top.astype(BF16)
            band_send[1, c, :, lanes] = bottom.astype(BF16)

    def band_copy(i):
        return pltpu.make_async_remote_copy(
            src_ref=band_send.at[i], dst_ref=band_recv.at[1 - i],
            send_sem=bs.at[i], recv_sem=br.at[1 - i],
            device_id=(above if i == 0 else below, me), device_id_type=MESH,
        )

    band_copies = [band_copy(i) for i in range(2)]
    for c in band_copies:
        c.start()
    for p in peers:
        gradient_arrival(p, 0).wait_recv()
    for c in range(2):
        for m in range(BLOCKS):
            lanes = slice(m * W, (m + 1) * W)
            top = bottom = jnp.zeros((BAND, W), F32)
            for p in range(DEPTH):
                up = upward(p)
                from_halo = jnp.where(up, half_rows - (BAND + offs[p]), offs[p] - 1 - half_rows) >= 0
                mask = column_mask(p, m)
                certain = jnp.where(mask, grecv[0, p, c].astype(F32), 0.0)
                mixed = jnp.where(mask & ~from_halo, grecv[1, p, c].astype(F32), 0.0)
                top = top + jnp.where(up, certain, mixed)
                bottom = bottom + jnp.where(up, mixed, certain)
            out_ref[c, 0, :BAND, lanes] = top
            out_ref[c, 0, BAND:, lanes] = bottom
    for i, c in enumerate(band_copies):
        c.wait()
    for i in range(2):
        edge = slice(i * BAND, (i + 1) * BAND)
        out_ref[:, 0, edge, :] = out_ref[:, 0, edge, :] + band_recv[i].astype(F32)
    for h in range(2):
        for p in peers:
            window_copy(h, p).wait_send()
            gradient_copy(p, h).wait_send()


def shards(tile_count, transmission, probe_wave, fresnel_phase, measured, positions, extents):
    right, left = dft_matrices()
    any_spec = pl.BlockSpec(memory_space=pl.ANY)
    smem = pl.BlockSpec(memory_space=pltpu.SMEM)
    dma = pltpu.SemaphoreType.DMA

    def body(*refs):
        kernel(tile_count, *refs)

    return pl.pallas_call(
        body,
        out_shape=jax.ShapeDtypeStruct(transmission.shape, F32),
        in_specs=[smem, smem] + [any_spec] * 6,
        out_specs=pl.BlockSpec(memory_space=pltpu.VMEM),
        scratch_shapes=[
            pltpu.VMEM((2, STRIP, OW), F32),
            pltpu.VMEM((2, W, W), F32),
            pltpu.VMEM((W, W), F32),
            pltpu.VMEM((W, W), F32),
            pltpu.VMEM(right.shape, BF16),
            pltpu.VMEM(left.shape, BF16),
            pltpu.VMEM((W, W), F32),
            pltpu.VMEM((W, W), F32),
            pltpu.VMEM((DEPTH, 2, W, W), F32),
            pltpu.VMEM((2, 2, BAND, OW), BF16),
            pltpu.VMEM((2, 2, BAND, OW), BF16),
            pltpu.VMEM((2, DEPTH, 2, BAND, W), BF16),
            pltpu.VMEM((2, DEPTH, 2, BAND, W), BF16),
            pltpu.VMEM((2, DEPTH, 2, BAND, W), BF16),
            pltpu.VMEM((2, DEPTH, 2, BAND, W), BF16),
            pltpu.VMEM((2, 2, BAND, OW), BF16),
            pltpu.VMEM((2, 2, BAND, OW), BF16),
            dma((6,)), dma((2,)), dma((2,)), dma((2, DEPTH)), dma((2, DEPTH)),
            dma((2, DEPTH)), dma((2, DEPTH)), dma((2,)), dma((2,)),
        ],
        compiler_params=pltpu.CompilerParams(collective_id=0, has_side_effects=True),
    )(positions, extents, transmission, probe_wave, fresnel_phase, measured,
      jnp.asarray(right), jnp.asarray(left))


def solution(mesh):
    tile_count = mesh.shape["tile"]
    placed = (
        P(None, "depth", "tile", None),
        P(),
        P(),
        P("tile", None, None),
        P("tile", None),
        P("tile", None),
    )

    def body(*args):
        return shards(tile_count, *args)

    return jax.shard_map(
        body,
        mesh=mesh,
        in_specs=placed,
        out_specs=P(None, "depth", "tile", None),
        check_vma=False,
    )
```

time: 125 us -> 48.6 us (0.39)
  the two profiles are of different devices: /device:TPU:128 before, /device:TPU:64 now
where the time goes in v1:
time: 48.6 us; the launch traced here: 48.4 us
  Pallas kernels  45.2 us (93%)
  local copies, waits for them, and re-layouts  3.2 us (7%)
    pallas_call x1, Pallas kernels, shards(): pl.pallas_call(body, out_shape=jax.ShapeDtypeStruct(transmission.shape, F...  45.2 us
    unnamed x2, local copies, waits for them, and re-layouts  3.2 us

profile of v1, /device:TPU:64, one launch (start us, length us, event | category | flops | bytes accessed | tf_op | source)
XLA Modules:
  0.0 48.4 jit_solution(11971492603868986331)
XLA Ops:
  0.0 1.3 %copy.9.refs_0_ = s32[4,2]{1,0:T(4,128)} copy(s32[4,2]{0,1:T(2,128)} %param.12) | data formatting | bytes 64 | tf_op args[4]
  1.3 45.2 %shard_map.82 = f32[2,1,128,512]{3,2,1,0:T(8,128)} custom-call(s32[4,2]{1,0:T(4,128)} %copy.9.refs_0_, s32[1,2]{1,0:T(1,128)} %refs_1_.1, f32[2,1,128,512]{3,2,1,0:T(8,128)} %refs_2_.1, f32[2,128,128]{2,1,0:T(8,128)} %refs_3_.1, f32[128,128]{1,0:T(8,128)} %refs_4_.1, f32[4,128,128]{2,1,0:T(8,128)} %refs_5_.1, bf16[2,768,256]{2,1,0:T(8,128)(2,1)} %constant.4.clone.refs_6_, ...), custom_call_target="tpu_custom_call" | custom-call | tf_op jit(solution)/shard_map/pallas_call | solution.py:322
  46.5 1.9 %copy.11 = f32[2,1,128,512]{3,2,1,0:T(8,128)} copy(f32[2,1,128,512]{3,2,1,0:T(8,128)} %shard_map.82) | data formatting | bytes 1048576

commit v2 on v1

--- a/solution.py
+++ b/solution.py
@@ -14,6 +14,7 @@
 OW = 512
 BLOCKS = OW // W
 DEPTH = 4
+RUN = 16
 F32 = jnp.float32
 BF16 = jnp.bfloat16
 MESH = pl.DeviceIdType.MESH
@@ -41,8 +42,8 @@
     pos_ref, ext_ref, tr_hbm, probe_hbm, phase_hbm, meas_hbm, right_hbm, left_hbm,
     out_ref,
     tr, probe, phase, meas, right, left, gcos, gsin, waves,
-    halo_send, halo, wsend, wrecv, gsend, grecv, band_send, band_recv,
-    local_sem, hs, hr, ws, wr, gs, gr, bs, br,
+    halo_send, halo, wsend, wrecv, gsend, grecv, band_send, band_recv, far_send, far_recv, col_send, col_recv,
+    local_sem, hs, hr, ws, wr, gs, gr, bs, br, fs, fr, cs, cr,
 ):
     t = lax.axis_index("tile")
     me = lax.axis_index("depth")
@@ -50,9 +51,28 @@
     below = lax.rem(t + 1, tile_count)
     peers = [lax.rem(me + j, DEPTH) for j in range(1, DEPTH)]
 
+    sides = (above, below)
+
+    def at_end(tile):
+        place = lax.rem(tile, RUN)
+        return (place == 0) | (place == RUN - 1)
+
+    end_me = at_end(t)
+    end_side = (at_end(above), at_end(below))
+
     barrier = pltpu.get_barrier_semaphore()
-    pl.semaphore_signal(barrier, inc=1, device_id=(above, me), device_id_type=MESH)
-    pl.semaphore_signal(barrier, inc=1, device_id=(below, me), device_id_type=MESH)
+    for side in sides:
+        pl.semaphore_signal(barrier, inc=1, device_id=(side, me), device_id_type=MESH)
+    expected = 2 + len(peers)
+    for i in range(2):
+        wide = end_me | end_side[i]
+        expected = expected + jnp.where(wide, len(peers), 0)
+
+        @pl.when(wide)
+        def _():
+            for p in peers:
+                pl.semaphore_signal(barrier, inc=1, device_id=(sides[i], p), device_id_type=MESH)
+
     for p in peers:
         pl.semaphore_signal(barrier, inc=1, device_id=(t, p), device_id_type=MESH)
 
@@ -69,10 +89,10 @@
 
     def offset_of(p):
         rows = STRIP * tile_count
-        return lax.rem(pos_ref[p, 0] - t * STRIP + (rows + BAND), rows) - BAND
+        return lax.rem(pos_ref[0, p] - t * STRIP + (rows + BAND), rows) - BAND
 
     offs = [offset_of(p) for p in range(DEPTH)]
-    cols = [pos_ref[p, 1] for p in range(DEPTH)]
+    cols = [pos_ref[1, p] for p in range(DEPTH)]
 
     half_rows = lax.broadcasted_iota(jnp.int32, (BAND, W), 0)
     half_lanes = lax.broadcasted_iota(jnp.int32, (BAND, W), 1)
@@ -97,7 +117,13 @@
                 total = jnp.where(column_mask(p, m), block, total)
             wsend[0, p, c] = total.astype(BF16)
 
-    pl.semaphore_wait(barrier, 2 + len(peers))
+    which = lax.broadcasted_iota(jnp.int32, (8, W), 0)
+    columns = which * 0
+    for p in range(DEPTH):
+        columns = jnp.where(which == p, cols[p], columns)
+    col_send[...] = columns.astype(F32)
+
+    pl.semaphore_wait(barrier, expected)
 
     def halo_copy(i):
         return pltpu.make_async_remote_copy(
@@ -127,11 +153,23 @@
         window_copy(0, p).start()
     wrecv[0, me] = wsend[0, me]
 
+    def column_copy(i):
+        return pltpu.make_async_remote_copy(
+            src_ref=col_send, dst_ref=col_recv.at[1 - i],
+            send_sem=cs.at[i], recv_sem=cr.at[1 - i],
+            device_id=(sides[i], me), device_id_type=MESH,
+        )
+
+    @pl.when(end_me)
+    def _():
+        for i in range(2):
+            column_copy(i).start()
+
     fetches[2].wait()
     gcos[...] = jnp.cos(phase[...])
     gsin[...] = jnp.sin(phase[...])
     my_off = offset_of(me)
-    my_col = pos_ref[me, 1]
+    my_col = pos_ref[1, me]
     rows = lax.broadcasted_iota(jnp.int32, (W, W), 0)
     extended = my_off + ((rows - my_off + W) & (W - 1))
     inside = (extended >= -ext_ref[0, 0]) & (extended < STRIP + ext_ref[0, 1])
@@ -218,13 +256,27 @@
     misfit = re * re + im * im - meas[...]
     re, im = transform(misfit * re, misfit * im, True, False)
 
-    up_full = (rows * 0 + my_off) <= 0
+    from_halo_me = jnp.where(up_me, half_rows - (BAND + my_off), my_off - 1 - half_rows) >= 0
 
     def gradient_copy(k, h):
         return pltpu.make_async_remote_copy(
             src_ref=gsend.at[h, k], dst_ref=grecv.at[h, me],
             send_sem=gs.at[h, k], recv_sem=gr.at[h, me],
             device_id=(t, k), device_id_type=MESH,
+        )
+
+    def far_copy(i, k):
+        return pltpu.make_async_remote_copy(
+            src_ref=far_send.at[i, k], dst_ref=far_recv.at[1 - i, me],
+            send_sem=fs.at[i, k], recv_sem=fr.at[1 - i, me],
+            device_id=(sides[i], k), device_id_type=MESH,
+        )
+
+    def far_arrival(i, p):
+        return pltpu.make_async_remote_copy(
+            src_ref=far_send.at[i, p], dst_ref=far_recv.at[i, p],
+            send_sem=fs.at[i, p], recv_sem=fr.at[i, p],
+            device_id=(sides[i], p), device_id_type=MESH,
         )
 
     def gradient_arrival(p, h):
@@ -239,6 +291,17 @@
             re, im = propagate(re, im, True, False)
         w_re, w_im = waves[k, 0], waves[k, 1]
         terms = (w_re * re + w_im * im, w_re * im - w_im * re)
+
+        @pl.when(end_me)
+        def _():
+            for c in range(2):
+                mixed = jnp.where(up_me, terms[c][BAND:], terms[c][:BAND])
+                mixed = jnp.where(from_halo_me, mixed, 0.0)
+                far_send[0, k, c] = jnp.where(up_me, mixed, 0.0).astype(BF16)
+                far_send[1, k, c] = jnp.where(up_me, 0.0, mixed).astype(BF16)
+            for i in range(2):
+                far_copy(i, k).start()
+
         for c in range(2):
             lower, upper = terms[c][:BAND], terms[c][BAND:]
             gsend[1, k, c] = jnp.where(up_me, upper, lower).astype(BF16)
@@ -260,19 +323,6 @@
 
     for p in peers:
         gradient_arrival(p, 1).wait_recv()
-    for c in range(2):
-        for m in range(BLOCKS):
-            lanes = slice(m * W, (m + 1) * W)
-            top = bottom = jnp.zeros((BAND, W), F32)
-            for p in range(DEPTH):
-                up = upward(p)
-                from_halo = jnp.where(up, half_rows - (BAND + offs[p]), offs[p] - 1 - half_rows) >= 0
-                piece = jnp.where(from_halo & column_mask(p, m), grecv[1, p, c].astype(F32), 0.0)
-                top = top + jnp.where(up, piece, 0.0)
-                bottom = bottom + jnp.where(up, 0.0, piece)
-            band_send[0, c, :, lanes] = top.astype(BF16)
-            band_send[1, c, :, lanes] = bottom.astype(BF16)
-
     def band_copy(i):
         return pltpu.make_async_remote_copy(
             src_ref=band_send.at[i], dst_ref=band_recv.at[1 - i],
@@ -280,9 +330,23 @@
             device_id=(above if i == 0 else below, me), device_id_type=MESH,
         )
 
-    band_copies = [band_copy(i) for i in range(2)]
-    for c in band_copies:
-        c.start()
+    @pl.when(~end_me)
+    def _():
+        for c in range(2):
+            for m in range(BLOCKS):
+                lanes = slice(m * W, (m + 1) * W)
+                top = bottom = jnp.zeros((BAND, W), F32)
+                for p in range(DEPTH):
+                    up = upward(p)
+                    from_halo = jnp.where(up, half_rows - (BAND + offs[p]), offs[p] - 1 - half_rows) >= 0
+                    piece = jnp.where(from_halo & column_mask(p, m), grecv[1, p, c].astype(F32), 0.0)
+                    top = top + jnp.where(up, piece, 0.0)
+                    bottom = bottom + jnp.where(up, 0.0, piece)
+                band_send[0, c, :, lanes] = top.astype(BF16)
+                band_send[1, c, :, lanes] = bottom.astype(BF16)
+        for i in range(2):
+            band_copy(i).start()
+
     for p in peers:
         gradient_arrival(p, 0).wait_recv()
     for c in range(2):
@@ -299,11 +363,43 @@
                 bottom = bottom + jnp.where(up, mixed, certain)
             out_ref[c, 0, :BAND, lanes] = top
             out_ref[c, 0, BAND:, lanes] = bottom
-    for i, c in enumerate(band_copies):
-        c.wait()
+    lanes_f = half_lanes.astype(F32)
     for i in range(2):
         edge = slice(i * BAND, (i + 1) * BAND)
-        out_ref[:, 0, edge, :] = out_ref[:, 0, edge, :] + band_recv[i].astype(F32)
+
+        @pl.when(~end_side[i])
+        def _():
+            band_copy(1 - i).wait_recv()
+            out_ref[:, 0, edge, :] = out_ref[:, 0, edge, :] + band_recv[i].astype(F32)
+
+        @pl.when(end_side[i])
+        def _():
+            column_copy(1 - i).wait_recv()
+            for p in range(DEPTH):
+                far_arrival(i, p).wait_recv()
+            for m in range(BLOCKS):
+                lanes = slice(m * W, (m + 1) * W)
+                totals = [out_ref[c, 0, edge, lanes] for c in range(2)]
+                for p in range(DEPTH):
+                    start = col_recv[i, p:p + 1, :] - float(m * W)
+                    mask = (lanes_f >= start) & (lanes_f < start + float(W))
+                    for c in range(2):
+                        totals[c] = totals[c] + jnp.where(mask, far_recv[i, p, c].astype(F32), 0.0)
+                for c in range(2):
+                    out_ref[c, 0, edge, lanes] = totals[c]
+
+    @pl.when(~end_me)
+    def _():
+        for i in range(2):
+            band_copy(i).wait_send()
+
+    @pl.when(end_me)
+    def _():
+        for i in range(2):
+            column_copy(i).wait_send()
+            for k in range(DEPTH):
+                far_copy(i, k).wait_send()
+
     for h in range(2):
         for p in peers:
             window_copy(h, p).wait_send()
@@ -321,7 +417,7 @@
 
     return pl.pallas_call(
         body,
-        out_shape=jax.ShapeDtypeStruct(transmission.shape, F32),
+        out_shape=pltpu.VMEM(transmission.shape, F32),
         in_specs=[smem, smem] + [any_spec] * 6,
         out_specs=pl.BlockSpec(memory_space=pltpu.VMEM),
         scratch_shapes=[
@@ -342,11 +438,16 @@
             pltpu.VMEM((2, DEPTH, 2, BAND, W), BF16),
             pltpu.VMEM((2, 2, BAND, OW), BF16),
             pltpu.VMEM((2, 2, BAND, OW), BF16),
+            pltpu.VMEM((2, DEPTH, 2, BAND, W), BF16),
+            pltpu.VMEM((2, DEPTH, 2, BAND, W), BF16),
+            pltpu.VMEM((8, W), F32),
+            pltpu.VMEM((2, 8, W), F32),
             dma((6,)), dma((2,)), dma((2,)), dma((2, DEPTH)), dma((2, DEPTH)),
             dma((2, DEPTH)), dma((2, DEPTH)), dma((2,)), dma((2,)),
+            dma((2, DEPTH)), dma((2, DEPTH)), dma((2,)), dma((2,)),
         ],
-        compiler_params=pltpu.CompilerParams(collective_id=0, has_side_effects=True),
-    )(positions, extents, transmission, probe_wave, fresnel_phase, measured,
+        compiler_params=pltpu.CompilerParams(collective_id=0, has_side_effects=True, vmem_limit_bytes=66506752),
+    )(positions.T, extents, transmission, probe_wave, fresnel_phase, measured,
       jnp.asarray(right), jnp.asarray(left))
 
 

time: 48.6 us -> 41.7 us (0.86)
  Pallas kernels: 45.2 us -> 40.8 us
  local copies, waits for them, and re-layouts: 3.2 us -> 0.8 us
    pallas_call x1, Pallas kernels: 45.2 us -> 40.8 us  [shards(): pl.pallas_call(body, out_shape=pltpu.VMEM(transmission.shape, F32), in_sp...]
    unnamed x2 -> x1, local copies, waits for them, and re-layouts: 3.2 us -> 0.8 us
where the time goes in v2:
time: 41.7 us; the launch traced here: 41.6 us
  Pallas kernels  40.8 us (98%)
  local copies, waits for them, and re-layouts  0.8 us (2%)
    pallas_call x1, Pallas kernels, shards(): pl.pallas_call(body, out_shape=pltpu.VMEM(transmission.shape, F32), in_sp...  40.8 us

profile of v2, /device:TPU:64, one launch (start us, length us, event | category | flops | bytes accessed | tf_op | source)
XLA Modules:
  0.0 41.6 jit_solution(11955682279424967956)
XLA Ops:
  0.0 40.8 %shard_map.82 = f32[2,1,128,512]{3,2,1,0:T(8,128)S(1)} custom-call(s32[2,4]{1,0:T(2,128)} %bitcast.1, s32[1,2]{1,0:T(1,128)} %refs_1_.1, f32[2,1,128,512]{3,2,1,0:T(8,128)} %refs_2_.1, f32[2,128,128]{2,1,0:T(8,128)} %refs_3_.1, f32[128,128]{1,0:T(8,128)} %refs_4_.1, f32[4,128,128]{2,1,0:T(8,128)} %refs_5_.1, bf16[2,768,256]{2,1,0:T(8,128)(2,1)} %constant.4.clone.refs_6_, ...), custom_call_target="tpu_custom_call" | custom-call | tf_op jit(solution)/shard_map/pallas_call | solution.py:418
  40.8 0.8 %copy.10 = f32[2,1,128,512]{3,2,1,0:T(8,128)} copy(f32[2,1,128,512]{3,2,1,0:T(8,128)S(1)} %shard_map.82) | data formatting | bytes 1048576

commit v3 on v2

--- a/solution.py
+++ b/solution.py
@@ -15,6 +15,11 @@
 BLOCKS = OW // W
 DEPTH = 4
 RUN = 16
+PARTS = 2
+FORWARD = (3, 3)
+TURN = (2, 2)
+BACKWARD = (2, 2)
+PART = BAND // PARTS
 F32 = jnp.float32
 BF16 = jnp.bfloat16
 MESH = pl.DeviceIdType.MESH
@@ -39,10 +44,10 @@
 
 def kernel(
     tile_count,
-    pos_ref, ext_ref, tr_hbm, probe_hbm, phase_hbm, meas_hbm, right_hbm, left_hbm,
+    pos_hbm, ext_hbm, tr_hbm, probe_hbm, phase_hbm, meas_hbm, right_hbm, left_hbm,
     out_ref,
     tr, probe, phase, meas, right, left, gcos, gsin, waves,
-    halo_send, halo, wsend, wrecv, gsend, grecv, band_send, band_recv, far_send, far_recv, col_send, col_recv,
+    halo_send, halo, wsend, wrecv, gsend, grecv, band_send, band_recv, far_send, far_recv, col_send, col_recv, pos_ref, ext_ref,
     local_sem, hs, hr, ws, wr, gs, gr, bs, br, fs, fr, cs, cr,
 ):
     t = lax.axis_index("tile")
@@ -53,24 +58,26 @@
 
     sides = (above, below)
 
-    def at_end(tile):
+    def straight(tile):
         place = lax.rem(tile, RUN)
         return (place == 0) | (place == RUN - 1)
 
-    end_me = at_end(t)
-    end_side = (at_end(above), at_end(below))
+    out_straight = [straight(t)] * 2
+    in_straight = [straight(side) for side in sides]
+    even = lax.rem(lax.div(t, RUN), 2) == 0
+    urgent = jnp.where((lax.rem(t, RUN) == 0) == even, 1, 0)
 
     barrier = pltpu.get_barrier_semaphore()
     for side in sides:
         pl.semaphore_signal(barrier, inc=1, device_id=(side, me), device_id_type=MESH)
     expected = 2 + len(peers)
     for i in range(2):
-        wide = end_me | end_side[i]
-        expected = expected + jnp.where(wide, len(peers), 0)
-
-        @pl.when(wide)
-        def _():
-            for p in peers:
+        for p in peers:
+            wide = out_straight[i] | in_straight[i]
+            expected = expected + jnp.where(wide, 1, 0)
+
+            @pl.when(wide)
+            def _():
                 pl.semaphore_signal(barrier, inc=1, device_id=(sides[i], p), device_id_type=MESH)
 
     for p in peers:
@@ -83,9 +90,13 @@
         pltpu.make_async_copy(meas_hbm.at[me], meas, local_sem.at[3]),
         pltpu.make_async_copy(right_hbm, right, local_sem.at[4]),
         pltpu.make_async_copy(left_hbm, left, local_sem.at[5]),
+        pltpu.make_async_copy(pos_hbm, pos_ref, local_sem.at[6]),
+        pltpu.make_async_copy(ext_hbm, ext_ref, local_sem.at[7]),
     ]
-    for f in fetches:
-        f.start()
+    for i in (6, 7, 0):
+        fetches[i].start()
+    for f in fetches[6:]:
+        f.wait()
 
     def offset_of(p):
         rows = STRIP * tile_count
@@ -93,6 +104,7 @@
 
     offs = [offset_of(p) for p in range(DEPTH)]
     cols = [pos_ref[1, p] for p in range(DEPTH)]
+    order = list(reversed(peers)) + [me]
 
     half_rows = lax.broadcasted_iota(jnp.int32, (BAND, W), 0)
     half_lanes = lax.broadcasted_iota(jnp.int32, (BAND, W), 1)
@@ -107,15 +119,6 @@
     fetches[0].wait()
     for i in range(2):
         halo_send[i] = tr[:, i * BAND:(i + 1) * BAND, :].astype(BF16)
-
-    for p in range(DEPTH):
-        up = upward(p)
-        for c in range(2):
-            total = jnp.zeros((BAND, W), F32)
-            for m in range(BLOCKS):
-                block = jnp.where(up, tr[c, :BAND, m * W:(m + 1) * W], tr[c, BAND:, m * W:(m + 1) * W])
-                total = jnp.where(column_mask(p, m), block, total)
-            wsend[0, p, c] = total.astype(BF16)
 
     which = lax.broadcasted_iota(jnp.int32, (8, W), 0)
     columns = which * 0
@@ -125,33 +128,60 @@
 
     pl.semaphore_wait(barrier, expected)
 
-    def halo_copy(i):
-        return pltpu.make_async_remote_copy(
-            src_ref=halo_send.at[i], dst_ref=halo.at[1 - i],
-            send_sem=hs.at[i], recv_sem=hr.at[1 - i],
-            device_id=(above if i == 0 else below, me), device_id_type=MESH,
-        )
+    def part_rows(q):
+        return slice(q * PART, (q + 1) * PART)
+
+    def halo_copy(i, q):
+        return pltpu.make_async_remote_copy(
+            src_ref=halo_send.at[i, :, part_rows(q)], dst_ref=halo.at[1 - i, :, part_rows(q)],
+            send_sem=hs.at[i, q], recv_sem=hr.at[1 - i, q],
+            device_id=(sides[i], me), device_id_type=MESH,
+        )
+
+    def window_part(ref, h, k):
+        return ref.at[0, k] if h == 0 else ref.at[1, k, :, part_rows(h - 1)]
 
     def window_copy(h, p):
         return pltpu.make_async_remote_copy(
-            src_ref=wsend.at[h, p], dst_ref=wrecv.at[h, me],
+            src_ref=window_part(wsend, h, p), dst_ref=window_part(wrecv, h, me),
             send_sem=ws.at[h, p], recv_sem=wr.at[h, me],
             device_id=(t, p), device_id_type=MESH,
         )
 
     def window_arrival(h, k):
         return pltpu.make_async_remote_copy(
-            src_ref=wsend.at[h, k], dst_ref=wrecv.at[h, k],
+            src_ref=window_part(wsend, h, k), dst_ref=window_part(wrecv, h, k),
             send_sem=ws.at[h, k], recv_sem=wr.at[h, k],
             device_id=(t, k), device_id_type=MESH,
         )
 
-    halo_copies = [halo_copy(i) for i in range(2)]
-    for c in halo_copies:
-        c.start()
-    for p in reversed(peers):
-        window_copy(0, p).start()
-    wrecv[0, me] = wsend[0, me]
+    for q in range(PARTS):
+        for i in range(2):
+            halo_copy(i, q).start()
+    for i in range(1, 6):
+        fetches[i].start()
+
+    def cut_masks(p):
+        start = pos_ref[1, p]
+        shift = offset_of(p)
+        up = (half_rows * 0 + shift) <= 0
+        outside = jnp.where(up, half_rows - (BAND + shift), shift - 1 - half_rows) >= 0
+        lanes = [(half_lanes + m * W >= start) & (half_lanes + m * W < start + W) for m in range(BLOCKS)]
+        return up, outside, lanes
+
+    for p in order:
+        up, _, picks = cut_masks(p)
+        for c in range(2):
+            total = jnp.zeros((BAND, W), F32)
+            for m in range(BLOCKS):
+                lanes = slice(m * W, (m + 1) * W)
+                total = jnp.where(picks[m], jnp.where(up, tr[c, :BAND, lanes], tr[c, BAND:, lanes]), total)
+            if p is me:
+                wrecv[0, me, c] = total.astype(BF16)
+            else:
+                wsend[0, p, c] = total.astype(BF16)
+        if p is not me:
+            window_copy(0, p).start()
 
     def column_copy(i):
         return pltpu.make_async_remote_copy(
@@ -160,9 +190,9 @@
             device_id=(sides[i], me), device_id_type=MESH,
         )
 
-    @pl.when(end_me)
-    def _():
-        for i in range(2):
+    for i in range(2):
+        @pl.when(out_straight[i])
+        def _():
             column_copy(i).start()
 
     fetches[2].wait()
@@ -179,23 +209,25 @@
         turned = pltpu.roll(turned, my_col & (W - 1), 1)
         waves[0, c] = jnp.where(inside, turned, 0.0)
 
-    for c in halo_copies:
-        c.wait()
-    for p in range(DEPTH):
-        up = upward(p)
-        from_halo = jnp.where(up, half_rows - (BAND + offs[p]), offs[p] - 1 - half_rows) >= 0
-        for c in range(2):
-            total = jnp.zeros((BAND, W), F32)
-            for m in range(BLOCKS):
-                lanes = slice(m * W, (m + 1) * W)
-                outer = jnp.where(up, halo[0, c, :, lanes].astype(F32), halo[1, c, :, lanes].astype(F32))
-                inner = jnp.where(up, tr[c, BAND:, lanes], tr[c, :BAND, lanes])
-                block = jnp.where(from_halo, outer, inner)
-                total = jnp.where(column_mask(p, m), block, total)
-            wsend[1, p, c] = total.astype(BF16)
-    for p in reversed(peers):
-        window_copy(1, p).start()
-    wrecv[1, me] = wsend[1, me]
+    for q in range(PARTS):
+        for i in range(2):
+            halo_copy(i, q).wait_recv()
+        for p in order:
+            up, outside, picks = cut_masks(p)
+            up, outside = up[part_rows(q)], outside[part_rows(q)]
+            for c in range(2):
+                total = jnp.zeros((PART, W), F32)
+                for m in range(BLOCKS):
+                    lanes = slice(m * W, (m + 1) * W)
+                    outer = jnp.where(up, halo[0, c, part_rows(q), lanes].astype(F32), halo[1, c, part_rows(q), lanes].astype(F32))
+                    inner = jnp.where(up, tr[c, BAND + q * PART:BAND + (q + 1) * PART, lanes], tr[c, part_rows(q), lanes])
+                    total = jnp.where(picks[m][part_rows(q)], jnp.where(outside, outer, inner), total)
+                if p is me:
+                    wrecv[1, me, c, part_rows(q)] = total.astype(BF16)
+                else:
+                    wsend[1, p, c, part_rows(q)] = total.astype(BF16)
+            if p is not me:
+                window_copy(q + 1, p).start()
 
     for i in (3, 4, 5):
         fetches[i].wait()
@@ -211,35 +243,36 @@
                 [jnp.where(up_me, certain, mixed), jnp.where(up_me, mixed, certain)], axis=0))
         return both
 
-    def split(x, exact):
+    def parts_of(x, products):
         high = x.astype(BF16)
-        if not exact:
-            return high, None
-        return high, (x - high.astype(F32)).astype(BF16)
-
-    def transform(re, im, inverse, exact):
+        parts = [high] * min(products, 2)
+        if products == 3:
+            parts.append((x - high.astype(F32)).astype(BF16))
+        return parts
+
+    def transform(re, im, inverse, products):
         d = 1 if inverse else 0
-        high, low = split(jnp.concatenate([re, im], axis=1), exact)
-        parts = [high, high] + ([low] if exact else [])
-        depth = len(parts) * 2 * W
-        u = jnp.dot(jnp.concatenate(parts, axis=1), right[d, :depth, :], preferred_element_type=F32)
-        high, low = split(jnp.concatenate([u[:, :W], u[:, W:]], axis=0), exact)
-        parts = [high, high] + ([low] if exact else [])
-        v = jnp.dot(left[d, :, :depth], jnp.concatenate(parts, axis=0), preferred_element_type=F32)
+        n_right, n_left = products
+        x = jnp.concatenate([re, im], axis=1)
+        u = jnp.dot(jnp.concatenate(parts_of(x, n_right), axis=1), right[d, :n_right * 2 * W, :],
+                    preferred_element_type=F32)
+        x = jnp.concatenate([u[:, :W], u[:, W:]], axis=0)
+        v = jnp.dot(left[d, :, :n_left * 2 * W], jnp.concatenate(parts_of(x, n_left), axis=0),
+                    preferred_element_type=F32)
         return v[:W], v[W:]
 
-    def propagate(re, im, conjugate, exact):
-        re, im = transform(re, im, False, exact)
+    def propagate(re, im, conjugate, products):
+        re, im = transform(re, im, False, products)
         co, si = gcos[...], gsin[...]
         if conjugate:
             re, im = re * co + im * si, im * co - re * si
         else:
             re, im = re * co - im * si, im * co + re * si
-        return transform(re, im, True, exact)
+        return transform(re, im, True, products)
 
     re = im = None
     for k in range(DEPTH):
-        for h in range(2):
+        for h in range(1 + PARTS):
             @pl.when(me != k)
             def _():
                 window_arrival(h, k).wait_recv()
@@ -251,10 +284,10 @@
             waves[k, 1] = im
         re, im = re * o_re - im * o_im, re * o_im + im * o_re
         if k + 1 < DEPTH:
-            re, im = propagate(re, im, False, True)
-    re, im = transform(re, im, False, True)
+            re, im = propagate(re, im, False, FORWARD)
+    re, im = transform(re, im, False, FORWARD)
     misfit = re * re + im * im - meas[...]
-    re, im = transform(misfit * re, misfit * im, True, False)
+    re, im = transform(misfit * re, misfit * im, True, TURN)
 
     from_halo_me = jnp.where(up_me, half_rows - (BAND + my_off), my_off - 1 - half_rows) >= 0
 
@@ -269,7 +302,7 @@
         return pltpu.make_async_remote_copy(
             src_ref=far_send.at[i, k], dst_ref=far_recv.at[1 - i, me],
             send_sem=fs.at[i, k], recv_sem=fr.at[1 - i, me],
-            device_id=(sides[i], k), device_id_type=MESH,
+            device_id=(jnp.where(i == 0, above, below), k), device_id_type=MESH,
         )
 
     def far_arrival(i, p):
@@ -288,19 +321,18 @@
 
     for k in reversed(range(DEPTH)):
         if k + 1 < DEPTH:
-            re, im = propagate(re, im, True, False)
+            re, im = propagate(re, im, True, BACKWARD)
         w_re, w_im = waves[k, 0], waves[k, 1]
         terms = (w_re * re + w_im * im, w_re * im - w_im * re)
 
-        @pl.when(end_me)
+        @pl.when(straight(t))
         def _():
             for c in range(2):
                 mixed = jnp.where(up_me, terms[c][BAND:], terms[c][:BAND])
                 mixed = jnp.where(from_halo_me, mixed, 0.0)
                 far_send[0, k, c] = jnp.where(up_me, mixed, 0.0).astype(BF16)
                 far_send[1, k, c] = jnp.where(up_me, 0.0, mixed).astype(BF16)
-            for i in range(2):
-                far_copy(i, k).start()
+            far_copy(urgent, k).start()
 
         for c in range(2):
             lower, upper = terms[c][:BAND], terms[c][BAND:]
@@ -312,6 +344,10 @@
             gradient_copy(k, 1).start()
             gradient_copy(k, 0).start()
 
+        @pl.when(straight(t))
+        def _():
+            far_copy(1 - urgent, k).start()
+
         @pl.when(me == k)
         def _():
             grecv[1, me] = gsend[1, k]
@@ -330,21 +366,21 @@
             device_id=(above if i == 0 else below, me), device_id_type=MESH,
         )
 
-    @pl.when(~end_me)
-    def _():
-        for c in range(2):
-            for m in range(BLOCKS):
-                lanes = slice(m * W, (m + 1) * W)
-                top = bottom = jnp.zeros((BAND, W), F32)
-                for p in range(DEPTH):
-                    up = upward(p)
-                    from_halo = jnp.where(up, half_rows - (BAND + offs[p]), offs[p] - 1 - half_rows) >= 0
-                    piece = jnp.where(from_halo & column_mask(p, m), grecv[1, p, c].astype(F32), 0.0)
-                    top = top + jnp.where(up, piece, 0.0)
-                    bottom = bottom + jnp.where(up, 0.0, piece)
-                band_send[0, c, :, lanes] = top.astype(BF16)
-                band_send[1, c, :, lanes] = bottom.astype(BF16)
-        for i in range(2):
+    for c in range(2):
+        for m in range(BLOCKS):
+            lanes = slice(m * W, (m + 1) * W)
+            top = bottom = jnp.zeros((BAND, W), F32)
+            for p in range(DEPTH):
+                up = upward(p)
+                from_halo = jnp.where(up, half_rows - (BAND + offs[p]), offs[p] - 1 - half_rows) >= 0
+                piece = jnp.where(from_halo & column_mask(p, m), grecv[1, p, c].astype(F32), 0.0)
+                top = top + jnp.where(up, piece, 0.0)
+                bottom = bottom + jnp.where(up, 0.0, piece)
+            band_send[0, c, :, lanes] = top.astype(BF16)
+            band_send[1, c, :, lanes] = bottom.astype(BF16)
+    for i in range(2):
+        @pl.when(~out_straight[i])
+        def _():
             band_copy(i).start()
 
     for p in peers:
@@ -367,12 +403,12 @@
     for i in range(2):
         edge = slice(i * BAND, (i + 1) * BAND)
 
-        @pl.when(~end_side[i])
+        @pl.when(~in_straight[i])
         def _():
             band_copy(1 - i).wait_recv()
             out_ref[:, 0, edge, :] = out_ref[:, 0, edge, :] + band_recv[i].astype(F32)
 
-        @pl.when(end_side[i])
+        @pl.when(in_straight[i])
         def _():
             column_copy(1 - i).wait_recv()
             for p in range(DEPTH):
@@ -388,28 +424,33 @@
                 for c in range(2):
                     out_ref[c, 0, edge, lanes] = totals[c]
 
-    @pl.when(~end_me)
-    def _():
-        for i in range(2):
+    for i in range(2):
+        @pl.when(~out_straight[i])
+        def _():
             band_copy(i).wait_send()
 
-    @pl.when(end_me)
-    def _():
-        for i in range(2):
+        @pl.when(out_straight[i])
+        def _():
             column_copy(i).wait_send()
-            for k in range(DEPTH):
+
+        for k in range(DEPTH):
+            @pl.when(out_straight[i])
+            def _():
                 far_copy(i, k).wait_send()
 
-    for h in range(2):
-        for p in peers:
+    for i in range(2):
+        for q in range(PARTS):
+            halo_copy(i, q).wait_send()
+    for p in peers:
+        for h in range(1 + PARTS):
             window_copy(h, p).wait_send()
+        for h in range(2):
             gradient_copy(p, h).wait_send()
 
 
 def shards(tile_count, transmission, probe_wave, fresnel_phase, measured, positions, extents):
     right, left = dft_matrices()
     any_spec = pl.BlockSpec(memory_space=pl.ANY)
-    smem = pl.BlockSpec(memory_space=pltpu.SMEM)
     dma = pltpu.SemaphoreType.DMA
 
     def body(*refs):
@@ -418,7 +459,7 @@
     return pl.pallas_call(
         body,
         out_shape=pltpu.VMEM(transmission.shape, F32),
-        in_specs=[smem, smem] + [any_spec] * 6,
+        in_specs=[any_spec] * 8,
         out_specs=pl.BlockSpec(memory_space=pltpu.VMEM),
         scratch_shapes=[
             pltpu.VMEM((2, STRIP, OW), F32),
@@ -442,7 +483,9 @@
             pltpu.VMEM((2, DEPTH, 2, BAND, W), BF16),
             pltpu.VMEM((8, W), F32),
             pltpu.VMEM((2, 8, W), F32),
-            dma((6,)), dma((2,)), dma((2,)), dma((2, DEPTH)), dma((2, DEPTH)),
+            pltpu.SMEM((2, DEPTH), jnp.int32),
+            pltpu.SMEM((1, 2), jnp.int32),
+            dma((8,)), dma((2, PARTS)), dma((2, PARTS)), dma((1 + PARTS, DEPTH)), dma((1 + PARTS, DEPTH)),
             dma((2, DEPTH)), dma((2, DEPTH)), dma((2,)), dma((2,)),
             dma((2, DEPTH)), dma((2, DEPTH)), dma((2,)), dma((2,)),
         ],

time: 41.7 us -> 39.1 us (0.938)
  the two profiles are of different devices: /device:TPU:64 before, /device:TPU:1 now
where the time goes in v3:
time: 39.1 us; the launch traced here: 39 us
  Pallas kernels  38.2 us (98%)
  local copies, waits for them, and re-layouts  0.8 us (2%)
    pallas_call x1, Pallas kernels, shards(): pl.pallas_call(body, out_shape=pltpu.VMEM(transmission.shape, F32), in_sp...  38.2 us
    unnamed x1, local copies, waits for them, and re-layouts  0.8 us

profile of v3, /device:TPU:1, one launch (start us, length us, event | category | flops | bytes accessed | tf_op | source)
XLA Modules:
  0.0 39.0 jit_solution(13771232022496403194)
XLA Ops:
  0.0 38.2 %shard_map.82 = f32[2,1,128,512]{3,2,1,0:T(8,128)S(1)} custom-call(s32[2,4]{1,0:T(2,128)} %bitcast.1, s32[1,2]{1,0:T(1,128)} %refs_1_.1, f32[2,1,128,512]{3,2,1,0:T(8,128)} %refs_2_.1, f32[2,128,128]{2,1,0:T(8,128)} %refs_3_.1, f32[128,128]{1,0:T(8,128)} %refs_4_.1, f32[4,128,128]{2,1,0:T(8,128)} %refs_5_.1, bf16[2,768,256]{2,1,0:T(8,128)(2,1)} %constant.4.clone.refs_6_, ...), custom_call_target="tpu_custom_call" | custom-call | tf_op jit(solution)/shard_map/pallas_call | solution.py:459
  38.2 0.8 %copy.10 = f32[2,1,128,512]{3,2,1,0:T(8,128)} copy(f32[2,1,128,512]{3,2,1,0:T(8,128)S(1)} %shard_map.82) | data formatting | bytes 1048576

commit v4 on v3

--- a/solution.py
+++ b/solution.py
@@ -16,7 +16,8 @@
 DEPTH = 4
 RUN = 16
 PARTS = 2
-FORWARD = (3, 3)
+LATER = (0, 1)
+FORWARD = (3, 2)
 TURN = (2, 2)
 BACKWARD = (2, 2)
 PART = BAND // PARTS
@@ -342,7 +343,8 @@
         @pl.when(me != k)
         def _():
             gradient_copy(k, 1).start()
-            gradient_copy(k, 0).start()
+            if k not in LATER:
+                gradient_copy(k, 0).start()
 
         @pl.when(straight(t))
         def _():
@@ -356,6 +358,11 @@
         if k > 0:
             o_re, o_im = layer(k)
             re, im = o_re * re + o_im * im, o_re * im - o_im * re
+
+    for k in LATER:
+        @pl.when(me != k)
+        def _():
+            gradient_copy(k, 0).start()
 
     for p in peers:
         gradient_arrival(p, 1).wait_recv()

time: 39.1 us -> 38.6 us (0.987)
  Pallas kernels: 38.2 us -> 37.6 us
    pallas_call x1, Pallas kernels: 38.2 us -> 37.6 us  [shards(): pl.pallas_call(body, out_shape=pltpu.VMEM(transmission.shape, F32), in_sp...]
where the time goes in v4:
time: 38.6 us; the launch traced here: 38.4 us
  Pallas kernels  37.6 us (97%)
  local copies, waits for them, and re-layouts  0.8 us (2%)
    pallas_call x1, Pallas kernels, shards(): pl.pallas_call(body, out_shape=pltpu.VMEM(transmission.shape, F32), in_sp...  37.6 us
    unnamed x1, local copies, waits for them, and re-layouts  0.8 us

profile of v4, /device:TPU:1, one launch (start us, length us, event | category | flops | bytes accessed | tf_op | source)
XLA Modules:
  0.0 38.4 jit_solution(8807626973096850642)
XLA Ops:
  0.0 37.6 %shard_map.82 = f32[2,1,128,512]{3,2,1,0:T(8,128)S(1)} custom-call(s32[2,4]{1,0:T(2,128)} %bitcast.1, s32[1,2]{1,0:T(1,128)} %refs_1_.1, f32[2,1,128,512]{3,2,1,0:T(8,128)} %refs_2_.1, f32[2,128,128]{2,1,0:T(8,128)} %refs_3_.1, f32[128,128]{1,0:T(8,128)} %refs_4_.1, f32[4,128,128]{2,1,0:T(8,128)} %refs_5_.1, bf16[2,768,256]{2,1,0:T(8,128)(2,1)} %constant.4.clone.refs_6_, ...), custom_call_target="tpu_custom_call" | custom-call | tf_op jit(solution)/shard_map/pallas_call | solution.py:466
  37.6 0.8 %copy.10 = f32[2,1,128,512]{3,2,1,0:T(8,128)} copy(f32[2,1,128,512]{3,2,1,0:T(8,128)S(1)} %shard_map.82) | data formatting | bytes 1048576

commit v5 on v4

--- a/solution.py
+++ b/solution.py
@@ -16,7 +16,7 @@
 DEPTH = 4
 RUN = 16
 PARTS = 2
-LATER = (0, 1)
+LATER = (0, 1, 2)
 FORWARD = (3, 2)
 TURN = (2, 2)
 BACKWARD = (2, 2)

time: 38.6 us -> 38.6 us (level)
  the two profiles are of different devices: /device:TPU:1 before, /device:TPU:64 now
where the time goes in v5:
time: 38.6 us; the launch traced here: 38.4 us
  Pallas kernels  37.6 us (97%)
  local copies, waits for them, and re-layouts  0.8 us (2%)
    pallas_call x1, Pallas kernels, shards(): pl.pallas_call(body, out_shape=pltpu.VMEM(transmission.shape, F32), in_sp...  37.6 us
    unnamed x1, local copies, waits for them, and re-layouts  0.8 us

profile of v5, /device:TPU:64, one launch (start us, length us, event | category | flops | bytes accessed | tf_op | source)
XLA Modules:
  0.0 38.4 jit_solution(12838302368805268943)
XLA Ops:
  0.0 37.6 %shard_map.82 = f32[2,1,128,512]{3,2,1,0:T(8,128)S(1)} custom-call(s32[2,4]{1,0:T(2,128)} %bitcast.1, s32[1,2]{1,0:T(1,128)} %refs_1_.1, f32[2,1,128,512]{3,2,1,0:T(8,128)} %refs_2_.1, f32[2,128,128]{2,1,0:T(8,128)} %refs_3_.1, f32[128,128]{1,0:T(8,128)} %refs_4_.1, f32[4,128,128]{2,1,0:T(8,128)} %refs_5_.1, bf16[2,768,256]{2,1,0:T(8,128)(2,1)} %constant.4.clone.refs_6_, ...), custom_call_target="tpu_custom_call" | custom-call | tf_op jit(solution)/shard_map/pallas_call | solution.py:466
  37.6 0.8 %copy.10 = f32[2,1,128,512]{3,2,1,0:T(8,128)} copy(f32[2,1,128,512]{3,2,1,0:T(8,128)S(1)} %shard_map.82) | data formatting | bytes 1048576
